TPU v7x, 512 devices: a whole 4x4x16 slice. The times are simulated.
512 devices in a mesh: dp: 8 (over y, core), ctx: 64 (over z, x).
Axes of the slice: x: 4, y: 4, z: 16, core: 2. Of those that a mesh axis runs over, the one named last changes fastest.
Arguments:
- queries: bfloat16 [8, 8192, 1024], P('dp', 'ctx'), may hold values from -6 to 6
- keys: bfloat16 [8, 8192, 1024], P('dp', 'ctx'), may hold values from -6 to 6
- values: bfloat16 [8, 8192, 1024], P('dp', 'ctx'), may hold values from -6 to 6
- log_decay: float32 [8, 8, 8192], P('dp', None, 'ctx'), may hold values from -2 to 0
- gain: float32 [1024], replicated, may hold values from 0.1 to 1.9
- out_grad: bfloat16 [8, 8192, 1024], P('dp', 'ctx'), may hold values from -16 to 16
Outputs:
- query_grad: bfloat16 [8, 8192, 1024], P('dp', 'ctx')
- key_grad: bfloat16 [8, 8192, 1024], P('dp', 'ctx')
- value_grad: bfloat16 [8, 8192, 1024], P('dp', 'ctx')
- gain_grad: float32 [1024], P('ctx')
All inputs are finite; a program needn't handle non-finite values.
Results may differ from a plain program's by a relative error of at most 0.0059.
Values sent between devices are 32-bit elements; how exact they have to be, the bound alone decides.
A program may use at most 128 MiB of HBM per device.

v0:
```python
import jax
import jax.numpy as jnp
from jax import lax
from jax.sharding import PartitionSpec as P

EPSILON = 1e-06


def prefix(part, axis, combine, identity, reverse):
    count = lax.axis_size(axis)
    place = lax.axis_index(axis)
    ahead = count - 1 - place if reverse else place
    gathered = jax.tree.map(lambda a: lax.all_gather(a, axis), part)
    state = jax.tree.map(lambda a, e: jnp.zeros_like(a) + jnp.asarray(e, a.dtype), part, identity)

    def one(step, state):
        source = count - 1 - step if reverse else step
        return combine(
            state, jax.tree.map(lambda a: lax.dynamic_index_in_dim(a, source, 0, False), gathered)
        )

    return lax.fori_loop(0, ahead, one, state)


def combine(earlier, latter):
    earlier_decay, earlier_state = earlier
    latter_decay, latter_state = latter
    return (
        earlier_decay * latter_decay,
        latter_decay[..., None, None] * earlier_state + latter_state,
    )


def causal_decay(cumulative):
    length = cumulative.shape[-1]
    causal = jnp.tril(jnp.ones((length, length), dtype=bool))
    spread = cumulative[..., :, None] - cumulative[..., None, :]
    return jnp.where(causal, jnp.exp(jnp.where(causal, spread, 0.0)), 0.0)


def body(queries, keys, values, log_decay, gain, out_grad):
    batch_rows, length, full_width = queries.shape
    head_count = log_decay.shape[1]
    head_size = full_width // head_count
    query_heads = queries.reshape(batch_rows, length, head_count, head_size)
    key_heads = keys.reshape(batch_rows, length, head_count, head_size)
    value_heads = values.reshape(batch_rows, length, head_count, head_size)
    cumulative = jnp.cumsum(log_decay, axis=2)
    from_start = jnp.exp(cumulative).transpose(0, 2, 1)[..., None]
    to_end = jnp.exp(cumulative[..., -1:] - cumulative).transpose(0, 2, 1)[..., None]
    key_decayed = (key_heads * to_end).astype(jnp.bfloat16)
    block_state = jnp.einsum(
        "bthi,bthj->bhij", key_decayed, value_heads, preferred_element_type=jnp.float32
    )
    block_decay = jnp.exp(cumulative[..., -1])
    start_decay = jnp.ones_like(block_decay)
    start_state = jnp.zeros_like(block_state)
    entering = prefix(
        (block_decay, block_state), "ctx", combine, (start_decay, start_state), False
    )[1]
    entering_half = entering.astype(jnp.bfloat16)
    decay_mask = causal_decay(cumulative)
    scores = jnp.einsum(
        "bthi,bshi->bhts", query_heads, key_heads, preferred_element_type=jnp.float32
    )
    weights = (scores * decay_mask).astype(jnp.bfloat16)
    attended = from_start * jnp.einsum(
        "bthi,bhij->bthj", query_heads, entering_half, preferred_element_type=jnp.float32
    )
    attended = attended + jnp.einsum(
        "bhts,bshj->bthj", weights, value_heads, preferred_element_type=jnp.float32
    )
    root_mean = jnp.sqrt(jnp.mean(attended * attended, axis=-1, keepdims=True) + EPSILON)
    normed = attended / root_mean
    upstream = out_grad.reshape(batch_rows, length, head_count, head_size).astype(jnp.float32)
    scaled_up = gain.reshape(head_count, head_size) * upstream
    attended_grad = (
        (scaled_up - normed * jnp.mean(scaled_up * normed, axis=-1, keepdims=True)) / root_mean
    ).astype(jnp.bfloat16)
    gain_terms = jnp.sum(upstream * normed, axis=(0, 1)).reshape(full_width)
    portion = full_width // lax.axis_size("ctx")
    summed = lax.psum(gain_terms, ("dp", "ctx"))
    gain_grad = lax.dynamic_slice_in_dim(summed, lax.axis_index("ctx") * portion, portion)
    grad_scores = jnp.einsum(
        "bthj,bshj->bhts", attended_grad, value_heads, preferred_element_type=jnp.float32
    )
    grad_weights = (grad_scores * decay_mask).astype(jnp.bfloat16)
    query_grad = from_start * jnp.einsum(
        "bthj,bhij->bthi", attended_grad, entering_half, preferred_element_type=jnp.float32
    )
    query_grad = query_grad + jnp.einsum(
        "bhts,bshi->bthi", grad_weights, key_heads, preferred_element_type=jnp.float32
    )
    query_decayed = (query_heads * from_start).astype(jnp.bfloat16)
    block_adjoint = jnp.einsum(
        "bthi,bthj->bhij", query_decayed, attended_grad, preferred_element_type=jnp.float32
    )
    returned = prefix(
        (block_decay, block_adjoint), "ctx", combine, (start_decay, start_state), True
    )[1]
    returned_half = returned.astype(jnp.bfloat16)
    key_grad = to_end * jnp.einsum(
        "bthj,bhij->bthi", value_heads, returned_half, preferred_element_type=jnp.float32
    )
    key_grad = key_grad + jnp.einsum(
        "bhts,bthi->bshi", grad_weights, query_heads, preferred_element_type=jnp.float32
    )
    value_grad = to_end * jnp.einsum(
        "bthi,bhij->bthj", key_heads, returned_half, preferred_element_type=jnp.float32
    )
    value_grad = value_grad + jnp.einsum(
        "bhts,bthj->bshj", weights, attended_grad, preferred_element_type=jnp.float32
    )
    return (
        query_grad.reshape(batch_rows, length, full_width).astype(jnp.bfloat16),
        key_grad.reshape(batch_rows, length, full_width).astype(jnp.bfloat16),
        value_grad.reshape(batch_rows, length, full_width).astype(jnp.bfloat16),
        gain_grad,
    )


def solution(mesh):
    in_specs = (
        P("dp", "ctx", None),
        P("dp", "ctx", None),
        P("dp", "ctx", None),
        P("dp", None, "ctx"),
        P(),
        P("dp", "ctx", None),
    )
    out_specs = (P("dp", "ctx", None), P("dp", "ctx", None), P("dp", "ctx", None), P("ctx"))
    return jax.shard_map(body, mesh=mesh, in_specs=in_specs, out_specs=out_specs, check_vma=False)
```

profile of v0, /device:TPU:24, one launch (start us, length us, event | category | flops | bytes accessed | tf_op | source)
XLA Modules:
  0.0 763.8 jit_solution(14405945986678790667)
XLA Ops:
  11.9 79.9 %all-gather = f32[64,8,1]{1,2,0:T(1,128)S(1)} all-gather(f32[1,8,1]{1,2,0:T(1,128)S(1)} %copy.61), channel_id=2, replica_groups=mesh['dp'=8,'ctx'=64] {'ctx'}, dimensions={0}, use_global_device_ids=true | all-gather | bytes 2080 | tf_op jit(solution)/shard_map/all_gather | solution.py:13
  94.9 215.6 %all-gather.6.cloned.1.call-done = f32[512,128,128]{2,1,0:T(8,128)} async-done(((f32[8,128,128]{2,1,0:T(8,128)}), f32[512,128,128]{2,1,0:T(8,128)}) %all-gather.6.cloned.1.call-update) | async-done | bytes 33554448 | tf_op jit(solution)/shard_map/all_gather | solution.py:13
  315.7 176.1 %psum.7 = f32[1024]{0:T(1024)S(1)} all-reduce(f32[1024]{0:T(1024)S(1)} %bitcast.158), channel_id=1, replica_groups=mesh['dp'=8,'ctx'=64] {'dp','ctx'}, use_global_device_ids=true, to_apply=%region_8.9 | all-reduce | flops 1024 | bytes 8192 | tf_op jit(solution)/shard_map/psum | solution.py:82
  492.8 184.0 %all-gather.8.cloned.1.call-done = f32[512,128,128]{2,1,0:T(8,128)} async-done(((f32[8,128,128]{2,1,0:T(8,128)}), f32[512,128,128]{2,1,0:T(8,128)}) %all-gather.8.cloned.1.call-update) | async-done | bytes 33554448 | tf_op jit(solution)/shard_map/all_gather | solution.py:13
  676.9 77.8 %while.27 = (s32[]{:T(128)}, f32[1,8,128,128]{3,2,1,0:T(8,128)S(1)}, s32[]{:T(128)}, f32[64,1,8]{2,1,0:T(1,128)S(1)}, f32[64,1,8,128,128]{4,3,2,1,0:T(8,128)}, /*index=5*/s32[]{:T(128)}, s32[]{:T(128)}, s32[]{:T(128)}, s32[]{:T(128)}) while((s32[]{:T(128)}, f32[1,8,128,128]{3,2,1,0:T(8,128)S(1)}, s32[]{:T(128)}, f32[64,1,8]{2,1,0:T(1,128)S(1)}, ...), condition=%wide.region_6.7_spmd, body=%wide.region_5.6_spmd.sunk | while | flops 262150 | bytes 1573107 | solution.py:22
  676.9 1.2 bitcast_add_fusion.5
  678.1 1.2 bitcast_add_fusion.5
  679.4 1.2 bitcast_add_fusion.5
  680.6 1.2 bitcast_add_fusion.5
  685.5 1.2 bitcast_add_fusion.5
  686.8 1.2 bitcast_add_fusion.5
  688.0 1.2 bitcast_add_fusion.5
  689.2 1.2 bitcast_add_fusion.5
  693.0 1.2 bitcast_add_fusion.5
  694.2 1.2 bitcast_add_fusion.5
  695.4 1.2 bitcast_add_fusion.5
  696.7 1.2 bitcast_add_fusion.5
  700.4 1.2 bitcast_add_fusion.5
  701.6 1.2 bitcast_add_fusion.5
  702.8 1.2 bitcast_add_fusion.5
  704.1 1.2 bitcast_add_fusion.5
  709.0 1.2 bitcast_add_fusion.5
  710.2 1.2 bitcast_add_fusion.5
  711.5 1.2 bitcast_add_fusion.5
  (146 shorter events, 69.0 us)
Async XLA Ops:
  7.2 303.3 %all-gather.6.cloned.1.call-start = ((), (), s32[]{:S(2)}) async-start(), calls=%async_computation | async-start | bytes 34078720 | tf_op jit(solution)/shard_map/all_gather | solution.py:13
  11.7 665.1 %all-gather.8.cloned.1.call-start = ((), (), s32[]{:S(2)}) async-start(), calls=%async_computation.1 | async-start | bytes 34078720 | tf_op jit(solution)/shard_map/all_gather | solution.py:13
Sparse Core Ops, SparseCore 0:
  11.8 298.5 all-gather.5
  314.1 362.6 all-gather.7
where the time goes:
time: 768 us; the launch traced here: 764 us
  waiting for transfers between devices  400 us (52%)
  blocking collectives  256 us (33%)
  other arithmetic  78 us (10%)
  between operations  14.2 us (2%)
  local copies, waits for them, and re-layouts  8.52 us (1%)
    all_gather x2, waiting for transfers between devices, prefix(): gathered = jax.tree.map(lambda a: lax.all_gather(a, axis), part)  400 us
    psum x1, blocking collectives, body(): summed = lax.psum(gain_terms, ('dp', 'ctx'))  176 us
    all_gather x1, blocking collectives, prefix(): gathered = jax.tree.map(lambda a: lax.all_gather(a, axis), part)  79.9 us
    add x63, other arithmetic, combine(): latter_decay[..., None, None] * earlier_state + latter_state  75 us
  transfers between devices with their start and end apart: 2, of which 2 were waited for; matrix products, arithmetic and copies ran while one was open for 1% of the time, Pallas kernels for 0%

commit v1 on v0

v1 whole, which is shorter than its diff:
```python
import functools

import jax
import jax.numpy as jnp
from jax import lax
from jax.experimental import pallas as pl
from jax.experimental.pallas import tpu as pltpu
from jax.sharding import PartitionSpec as P

EPSILON = 1e-06
HEADS = 8
E = 128
NX = 4
PER = HEADS // NX
AWAY = (2, 1, 3)
NEAR = (0, 1, 3, 2)
F32 = jnp.float32
BF16 = jnp.bfloat16
MESH = pl.DeviceIdType.MESH


def dot(a, b, ca, cb):
    return lax.dot_general(a, b, (((ca,), (cb,)), ((), ())), preferred_element_type=F32)


def kernel(nz, nd, q, k, v, ld, gain, og, qg, kg, vg, gg,
           fs, te, dm, wts, att, ag, kgi, vgi,
           dself, dx, drow, dz, st, xr, rt, zr, zp, zb, ex, eb,
           gt, gx, gxs, gz, gzs, gd,
           xs_s, xs_r, zs_s, zs_r, zb_s, zb_r, xb_s, xb_r,
           dx_s, dx_r, dz_s, dz_r, gd_s, gx_r, gz_r, gd_r):
    ch = E // nz
    c = lax.axis_index("ctx")
    me = lax.axis_index("dp")
    z = lax.div(c, NX)
    x = lax.rem(c, NX)

    def xat(n):
        return lax.rem(x + n, NX)

    def zat(n):
        return lax.rem(z + n, nz)

    def dat(n):
        return lax.rem(me + n, nd)

    def xdev(i):
        return {"ctx": z * NX + i}

    def zdev(i):
        return {"ctx": i * NX + x}

    def ddev(i):
        return {"dp": i}

    def rcopy(src, dst, ss, rs, dev):
        return pltpu.make_async_remote_copy(
            src_ref=src, dst_ref=dst, send_sem=ss, recv_sem=rs, device_id=dev, device_id_type=MESH
        )

    def each(count, f):
        def one(i, carry):
            f(i)
            return carry

        lax.fori_loop(1, count, one, 0)

    def rows(i):
        return pl.ds(pl.multiple_of(i * ch, ch), ch)

    def cols(h):
        return pl.ds(h * E if isinstance(h, int) else pl.multiple_of(h * E, E), E)

    barrier = pltpu.get_barrier_semaphore()
    for n in range(1, NX):
        pl.semaphore_signal(barrier, inc=1, device_id=xdev(xat(n)), device_id_type=MESH)
    each(nz, lambda i: pl.semaphore_signal(barrier, inc=1, device_id=zdev(zat(i)), device_id_type=MESH))
    each(nd, lambda i: pl.semaphore_signal(barrier, inc=1, device_id=ddev(dat(i)), device_id_type=MESH))

    first = lax.broadcasted_iota(jnp.int32, (E, E), 0)
    second = lax.broadcasted_iota(jnp.int32, (E, E), 1)
    upper = jnp.where(first <= second, 1.0, 0.0).astype(F32)
    causal = second <= first
    cum = lax.dot_general(
        ld[...], upper, (((1,), (0,)), ((), ())),
        precision=lax.Precision.HIGHEST, preferred_element_type=F32,
    )
    end = cum[:, E - 1:E]
    dself[...] = jnp.exp(jnp.broadcast_to(end, (HEADS, E)))
    cum_col = cum.T
    fs_col = jnp.exp(cum).T
    te_col = jnp.exp(end - cum).T
    for h in range(HEADS):
        fs[h] = jnp.broadcast_to(fs_col[:, h:h + 1], (E, E))
        te[h] = jnp.broadcast_to(te_col[:, h:h + 1], (E, E))

    for j in range(PER):
        for n in (2, 1, 3, 0):
            h = PER * xat(n) + j
            kd = (k[:, cols(h)].astype(F32) * te[h]).astype(BF16)
            state = dot(kd, v[:, cols(h)], 0, 0)
            if n:
                st[0, h] = state
            else:
                xr[0, j, x] = state
    dx[x] = dself[...]

    pl.semaphore_wait(barrier, NX - 1 + nz - 1 + nd - 1)

    def dx_copy(i, slot):
        return rcopy(dself, dx.at[slot], dx_s.at[i], dx_r.at[slot], xdev(i))

    def dz_copy(i, slot):
        return rcopy(drow, dz.at[slot], dz_s.at[i], dz_r.at[slot], zdev(i))

    def xs_copy(d, j, i, slot):
        return rcopy(st.at[d, PER * i + j], xr.at[d, j, slot], xs_s.at[j, i], xs_r.at[d, j, slot], xdev(i))

    def zs_copy(d, j, i, slot):
        return rcopy(rt.at[d, j, rows(i)], zr.at[d, j, slot], zs_s.at[j, i], zs_r.at[d, j, slot], zdev(i))

    def zb_copy(d, j, i, slot):
        return rcopy(zp.at[d, j, i], zb.at[d, j, rows(slot)], zb_s.at[j, i], zb_r.at[d, j, slot], zdev(i))

    def xb_copy(d, j, i, slot):
        return rcopy(
            ex.at[d, j, i], eb.at[d, PER * slot + j], xb_s.at[j, i], xb_r.at[d, j, slot], xdev(i)
        )

    def gx_copy(i, slot):
        return rcopy(gt, gx.at[slot], dx_s.at[i], gx_r.at[slot], xdev(i))

    def gz_copy(i, slot):
        return rcopy(gxs, gz.at[slot], dz_s.at[i], gz_r.at[slot], zdev(i))

    def gd_copy(i, slot):
        return rcopy(gzs, gd.at[slot], gd_s.at[i], gd_r.at[slot], ddev(i))

    for n in AWAY:
        dx_copy(xat(n), x).start()
    for j in range(PER):
        for n in AWAY:
            xs_copy(0, j, xat(n), x).start()

    def scan(d, fill):
        steps = range(NX) if d == 0 else range(NX - 1, -1, -1)
        for j in range(PER):
            for n in (1, 3, 2):
                xs_copy(d, j, xat(n), xat(n)).wait_recv()
            total = None
            for i in steps:
                part = xr[d, j, i]
                if total is None:
                    total = part
                else:
                    total = dx[i, pl.ds(PER * x + j, 1), :] * total + part
            rt[d, j] = total
            zr[d, j, z] = rt[d, j, rows(z)]
            each(nz, lambda i: zs_copy(d, j, zat(i), z).start())
            fill()
        for j in range(PER):
            each(nz, lambda i: zs_copy(d, j, zat(i), zat(i)).wait_recv())
            run = jnp.zeros((ch, E), F32)
            for s in range(nz):
                i = s if d == 0 else nz - 1 - s
                zp[d, j, i] = run
                if s < nz - 1:
                    run = dz[i, pl.ds(PER * x + j, 1), :] * run + zr[d, j, i]
            zb[d, j, rows(z)] = zp[d, j, z]
            each(nz, lambda i: zb_copy(d, j, zat(i), z).start())
            fill()
        for j in range(PER):
            each(nz, lambda i: zb_copy(d, j, zat(i), zat(i)).wait_recv())
            carried = zb[d, j]
            for s, i in enumerate(steps):
                ex[d, j, i] = carried
                if s < NX - 1:
                    carried = dx[i, pl.ds(PER * x + j, 1), :] * carried + xr[d, j, i]
            for n in AWAY:
                xb_copy(d, j, xat(n), x).start()
            eb[d, PER * x + j] = ex[d, j, x]

    def early(h):
        own = cum_col[:, h:h + 1] - cum[h:h + 1, :]
        mask = jnp.where(causal, jnp.exp(jnp.where(causal, own, 0.0)), 0.0)
        dm[h] = mask
        w = (dot(q[:, cols(h)], k[:, cols(h)], 1, 1) * mask).astype(BF16)
        wts[h] = w
        att[h] = dot(w, v[:, cols(h)], 1, 0)

    early(0)
    for n in AWAY:
        dx_copy(xat(n), xat(n)).wait_recv()
    drow[...] = dx[0] * dx[1] * dx[2] * dx[3]
    dz[z] = drow[...]
    each(nz, lambda i: dz_copy(zat(i), z).start())
    early(1)
    todo = [(2, 3), (4, 5), (6,), (7,)]

    def fill_early():
        for h in todo.pop(0):
            early(h)
        if len(todo) == 2:
            each(nz, lambda i: dz_copy(zat(i), zat(i)).wait_recv())

    scan(0, fill_early)

    for n in AWAY:
        dx_copy(xat(n), x).wait_send()
    each(nz, lambda i: dz_copy(zat(i), z).wait_send())
    for j in range(PER):
        for n in AWAY:
            xs_copy(0, j, xat(n), x).wait_send()
        each(nz, lambda i: zs_copy(0, j, zat(i), z).wait_send())
        each(nz, lambda i: zb_copy(0, j, zat(i), z).wait_send())

    for j in range(PER):
        for n in NEAR:
            i = xat(n)
            h = PER * i + j
            if n:
                xb_copy(0, j, i, i).wait_recv()
            eh = eb[0, h].astype(BF16)
            qh = q[:, cols(h)]
            start = fs[h]
            attended = start * dot(qh, eh, 1, 0) + att[h]
            inverse = lax.rsqrt(jnp.mean(attended * attended, axis=-1, keepdims=True) + EPSILON)
            normed = attended * inverse
            up = og[:, cols(h)].astype(F32)
            scaled = gain[pl.ds(h, 1), :] * up
            a = (
                (scaled - normed * jnp.mean(scaled * normed, axis=-1, keepdims=True)) * inverse
            ).astype(BF16)
            ag[h] = a
            qd = (qh.astype(F32) * start).astype(BF16)
            adjoint = dot(qd, a, 0, 0)
            if n:
                st[1, h] = adjoint
                xs_copy(1, j, i, x).start()
            else:
                xr[1, j, x] = adjoint
            gt[pl.ds(h, 1), :] = jnp.sum(up * normed, axis=0, keepdims=True)
    for n in AWAY:
        gx_copy(xat(n), x).start()
    gx[x] = gt[...]

    def late(h):
        a = ag[h]
        vh = v[:, cols(h)]
        gw = (dot(a, vh, 1, 1) * dm[h]).astype(BF16)
        eh = eb[0, h].astype(BF16)
        grad = fs[h] * dot(a, eh, 1, 1) + dot(gw, k[:, cols(h)], 1, 0)
        qg[:, cols(h)] = grad.astype(BF16)
        kgi[h] = dot(gw, q[:, cols(h)], 0, 0)
        vgi[h] = dot(wts[h], a, 0, 0)

    late(0)
    late(1)
    rest = [(2, 3), (4, 5), (6,), (7,)]

    def fill_late():
        for h in rest.pop(0):
            late(h)
        if len(rest) == 2:
            for n in AWAY:
                gx_copy(xat(n), xat(n)).wait_recv()
            gxs[...] = gx[0] + gx[1] + gx[2] + gx[3]
            each(nz, lambda i: gz_copy(zat(i), z).start())
            gz[z] = gxs[...]
        if len(rest) == 0:
            each(nz, lambda i: gz_copy(zat(i), zat(i)).wait_recv())
            gzs[...] = jnp.sum(gz[...], axis=0)
            each(nd, lambda i: gd_copy(dat(i), me).start())
            gd[me] = gzs[...]

    for j in range(PER):
        for n in AWAY:
            xb_copy(0, j, xat(n), x).wait_send()

    scan(1, fill_late)

    for j in range(PER):
        for n in NEAR:
            i = xat(n)
            h = PER * i + j
            if n:
                xb_copy(1, j, i, i).wait_recv()
            rh = eb[1, h].astype(BF16)
            stop = te[h]
            kg[:, cols(h)] = (stop * dot(v[:, cols(h)], rh, 1, 1) + kgi[h]).astype(BF16)
            vg[:, cols(h)] = (stop * dot(k[:, cols(h)], rh, 1, 0) + vgi[h]).astype(BF16)

    each(nd, lambda i: gd_copy(dat(i), dat(i)).wait_recv())
    gg[...] = jnp.sum(gd[...], axis=0)

    for n in AWAY:
        gx_copy(xat(n), x).wait_send()
    each(nz, lambda i: gz_copy(zat(i), z).wait_send())
    each(nd, lambda i: gd_copy(dat(i), me).wait_send())
    for j in range(PER):
        for n in AWAY:
            xs_copy(1, j, xat(n), x).wait_send()
            xb_copy(1, j, xat(n), x).wait_send()
        each(nz, lambda i: zs_copy(1, j, zat(i), z).wait_send())
        each(nz, lambda i: zb_copy(1, j, zat(i), z).wait_send())


def body(queries, keys, values, log_decay, gain, out_grad):
    nc = lax.axis_size("ctx")
    nd = lax.axis_size("dp")
    nz = nc // NX
    ch = E // nz
    width = HEADS * E

    def vm(*shape, dtype=F32):
        return pltpu.VMEM(shape, dtype)

    dma = lambda *shape: pltpu.SemaphoreType.DMA(shape)
    flat = lambda a: a.reshape(E, width)
    wide = jax.ShapeDtypeStruct((E, width), BF16)
    qg, kg, vg, gg = pl.pallas_call(
        functools.partial(kernel, nz, nd),
        out_shape=(wide, wide, wide, jax.ShapeDtypeStruct((HEADS, E), F32)),
        in_specs=[pl.BlockSpec(memory_space=pltpu.VMEM)] * 6,
        out_specs=tuple([pl.BlockSpec(memory_space=pltpu.VMEM)] * 4),
        scratch_shapes=[
            vm(HEADS, E, E), vm(HEADS, E, E), vm(HEADS, E, E),
            vm(HEADS, E, E, dtype=BF16), vm(HEADS, E, E), vm(HEADS, E, E, dtype=BF16),
            vm(HEADS, E, E), vm(HEADS, E, E),
            vm(HEADS, E), vm(NX, HEADS, E), vm(HEADS, E), vm(nz, HEADS, E),
            vm(2, HEADS, E, E), vm(2, PER, NX, E, E), vm(2, PER, E, E),
            vm(2, PER, nz, ch, E), vm(2, PER, nz, ch, E), vm(2, PER, E, E),
            vm(2, PER, NX, E, E), vm(2, HEADS, E, E),
            vm(HEADS, E), vm(NX, HEADS, E), vm(HEADS, E), vm(nz, HEADS, E),
            vm(HEADS, E), vm(nd, HEADS, E),
            dma(PER, NX), dma(2, PER, NX), dma(PER, nz), dma(2, PER, nz),
            dma(PER, nz), dma(2, PER, nz), dma(PER, NX), dma(2, PER, NX),
            dma(NX), dma(NX), dma(nz), dma(nz), dma(nd), dma(NX), dma(nz), dma(nd),
        ],
        compiler_params=pltpu.CompilerParams(
            collective_id=0, has_side_effects=True, vmem_limit_bytes=48 * 1024 * 1024
        ),
    )(
        flat(queries), flat(keys), flat(values), log_decay.reshape(HEADS, E),
        gain.reshape(HEADS, E), flat(out_grad),
    )
    portion = width // nc
    share = lax.dynamic_slice_in_dim(gg.reshape(width), lax.axis_index("ctx") * portion, portion)
    whole = lambda a: a.reshape(1, E, width)
    return whole(qg), whole(kg), whole(vg), share


def solution(mesh):
    in_specs = (
        P("dp", "ctx", None),
        P("dp", "ctx", None),
        P("dp", "ctx", None),
        P("dp", None, "ctx"),
        P(),
        P("dp", "ctx", None),
    )
    out_specs = (P("dp", "ctx", None), P("dp", "ctx", None), P("dp", "ctx", None), P("ctx"))
    return jax.shard_map(body, mesh=mesh, in_specs=in_specs, out_specs=out_specs, check_vma=False)
```

time: 768 us -> 88.1 us (0.11)
  waiting for transfers between devices: 400 us -> 0 us
  blocking collectives: 256 us -> 0 us
  Pallas kernels: 0 us -> 80 us
  other arithmetic: 78 us -> 0 us
  between operations: 14.2 us -> 0.67 us
    all_gather x2 -> x0, waiting for transfers between devices: 400 us -> none  [prefix(): gathered = jax.tree.map(lambda a: lax.all_gather(a, axis), part)]
    psum x1 -> x0, blocking collectives: 176 us -> none  [body(): summed = lax.psum(gain_terms, ('dp', 'ctx'))]
    pallas_call x0 -> x1, Pallas kernels: none -> 80 us  [body(): pl.pallas_call(functools.partial(kernel, nz, nd), out_shape=(wide, wide,...]
    all_gather x1 -> x0, blocking collectives: 79.9 us -> none  [prefix(): gathered = jax.tree.map(lambda a: lax.all_gather(a, axis), part)]
    add x63 -> x0, other arithmetic: 75 us -> none  [combine(): latter_decay[..., None, None] * earlier_state + latter_state]
  transfers between devices with their start and end apart: 2 -> 0, of which waited for: 2 -> 0; matrix products, arithmetic and copies ran while one was open for 1% -> 0% of each run, Pallas kernels for 0% -> 0%
where the time goes in v1:
time: 88.1 us; the launch traced here: 87.9 us
  Pallas kernels  80 us (91%)
  local copies, waits for them, and re-layouts  7.18 us (8%)
    pallas_call x1, Pallas kernels, body(): pl.pallas_call(functools.partial(kernel, nz, nd), out_shape=(wide, wide,...  80 us
    unnamed x15, local copies, waits for them, and re-layouts  6.59 us

profile of v1, /device:TPU:24, one launch (start us, length us, event | category | flops | bytes accessed | tf_op | source)
XLA Modules:
  0.0 87.9 jit_solution(12369414492011855429)
XLA Ops:
  0.6 0.0 copy-start.5
  0.6 0.0 copy-start.4
  0.7 0.7 copy-done.5
  1.3 0.0 copy-done.4
  1.3 0.0 copy-start
  1.3 0.9 %copy-done = bf16[1,128,1024]{2,1,0:T(8,128)(2,1)S(1)} copy-done((bf16[1,128,1024]{2,1,0:T(8,128)(2,1)S(1)}, bf16[1,128,1024]{2,1,0:T(8,128)(2,1)}, u32[]{:S(2)}) %copy-start) | copy-done | bytes 262168
  2.3 0.0 copy-start.1
  2.3 0.9 %copy-done.1 = bf16[1,128,1024]{2,1,0:T(8,128)(2,1)S(1)} copy-done((bf16[1,128,1024]{2,1,0:T(8,128)(2,1)S(1)}, bf16[1,128,1024]{2,1,0:T(8,128)(2,1)}, u32[]{:S(2)}) %copy-start.1) | copy-done | bytes 262168
  3.2 0.0 copy-start.2
  3.2 0.9 %copy-done.2 = bf16[1,128,1024]{2,1,0:T(8,128)(2,1)S(1)} copy-done((bf16[1,128,1024]{2,1,0:T(8,128)(2,1)S(1)}, bf16[1,128,1024]{2,1,0:T(8,128)(2,1)}, u32[]{:S(2)}) %copy-start.2) | copy-done | bytes 262168
  4.2 0.0 copy-start.3
  4.2 0.9 %copy-done.3 = bf16[1,128,1024]{2,1,0:T(8,128)(2,1)S(1)} copy-done((bf16[1,128,1024]{2,1,0:T(8,128)(2,1)S(1)}, bf16[1,128,1024]{2,1,0:T(8,128)(2,1)}, u32[]{:S(2)}) %copy-start.3) | copy-done | bytes 262168
  5.1 80.0 %shard_map.93 = (bf16[128,1024]{1,0:T(8,128)(2,1)S(1)}, bf16[128,1024]{1,0:T(8,128)(2,1)S(1)}, bf16[128,1024]{1,0:T(8,128)(2,1)S(1)}, f32[8,128]{1,0:T(8,128)S(1)}) custom-call(bf16[128,1024]{1,0:T(8,128)(2,1)S(1)} %bitcast.13, bf16[128,1024]{1,0:T(8,128)(2,1)S(1)} %bitcast.14, bf16[128,1024]{1,0:T(8,128)(2,1)S(1)} %bitcast.15, f32[8,128]{1,0:T(8,128)S(1)} %bitcast.17, ...), custom_call_target="tpu_custom_call" | custom-call | tf_op jit(solution)/shard_map/pallas_call | solution.py:321
  85.2 0.6 dynamic_slice.3
  85.7 0.7 copy.13
  86.5 0.7 copy.14
  87.2 0.7 copy.15
Async XLA Ops:
  0.6 0.7 copy-start.5
  0.6 0.7 copy-start.4
  1.3 0.9 %copy-start = (bf16[1,128,1024]{2,1,0:T(8,128)(2,1)S(1)}, bf16[1,128,1024]{2,1,0:T(8,128)(2,1)}, u32[]{:S(2)}) copy-start(bf16[1,128,1024]{2,1,0:T(8,128)(2,1)} %param.6) | copy-start | bytes 786436
  2.3 0.9 %copy-start.1 = (bf16[1,128,1024]{2,1,0:T(8,128)(2,1)S(1)}, bf16[1,128,1024]{2,1,0:T(8,128)(2,1)}, u32[]{:S(2)}) copy-start(bf16[1,128,1024]{2,1,0:T(8,128)(2,1)} %param.7) | copy-start | bytes 786436
  3.2 0.9 %copy-start.2 = (bf16[1,128,1024]{2,1,0:T(8,128)(2,1)S(1)}, bf16[1,128,1024]{2,1,0:T(8,128)(2,1)}, u32[]{:S(2)}) copy-start(bf16[1,128,1024]{2,1,0:T(8,128)(2,1)} %param.8) | copy-start | bytes 786436
  4.2 0.9 %copy-start.3 = (bf16[1,128,1024]{2,1,0:T(8,128)(2,1)S(1)}, bf16[1,128,1024]{2,1,0:T(8,128)(2,1)}, u32[]{:S(2)}) copy-start(bf16[1,128,1024]{2,1,0:T(8,128)(2,1)} %param.11) | copy-start | bytes 786436

commit v2 on v1

v2 whole, which is shorter than its diff:
```python
import functools

import jax
import jax.numpy as jnp
from jax import lax
from jax.experimental import pallas as pl
from jax.experimental.pallas import tpu as pltpu
from jax.sharding import PartitionSpec as P

EPSILON = 1e-06
HEADS = 8
E = 128
NX = 4
HALF = E // 2
PER = HEADS // NX
AWAY = (2, 1, 3)
NEAR = (0, 1, 3, 2)
F32 = jnp.float32
BF16 = jnp.bfloat16
MESH = pl.DeviceIdType.MESH


def dot(a, b, ca, cb):
    return lax.dot_general(a, b, (((ca,), (cb,)), ((), ())), preferred_element_type=F32)


def kernel(nz, nd, qi, ki, vi, ldi, gaini, ogi, qg, kg, vg, gg, q, k, v, og, ld, gain,
           fs, te, dm, wts, att, ag, kgi, vgi,
           dself, dx, drow, dz, st, xr, rt, zr, zp, zb, ex, eb,
           gt, gx, gxs, gz, gzs, gd,
           xs_s, xs_r, zs_s, zs_r, zb_s, zb_r, xb_s, xb_r,
           dx_s, dx_r, dz_s, dz_r, gd_s, gx_r, gz_r, gd_r, in_s):
    ch = E // nz
    c = lax.axis_index("ctx")
    me = lax.axis_index("dp")
    z = lax.div(c, NX)
    x = lax.rem(c, NX)

    def xat(n):
        return lax.rem(x + n, NX)

    def zat(n):
        return lax.rem(z + n, nz)

    def dat(n):
        return lax.rem(me + n, nd)

    def xdev(i):
        return {"ctx": z * NX + i}

    def zdev(i):
        return {"ctx": i * NX + x}

    def ddev(i):
        return {"dp": i}

    def rcopy(src, dst, ss, rs, dev):
        return pltpu.make_async_remote_copy(
            src_ref=src, dst_ref=dst, send_sem=ss, recv_sem=rs, device_id=dev, device_id_type=MESH
        )

    def each(count, f):
        def one(i, carry):
            f(i)
            return carry

        lax.fori_loop(1, count, one, 0)

    def far(f):
        def one(i, carry):
            f(zat(nz // 2 + ((i + 1) // 2) * (1 - 2 * (i % 2))))
            return carry

        lax.fori_loop(0, nz - 1, one, 0)

    def owners(p, f):
        def one(i, carry):
            near = (i + 1) // 2
            f(zat(nz // 2 + 2 * near * (1 - 2 * (i % 2)) + nz))
            return carry

        def other(i, carry):
            near = 2 * (i // 2) + 1
            f(zat(nz // 2 + near * (1 - 2 * (i % 2)) + nz))
            return carry

        same = (z + p + nz // 2) % 2 == 0

        @pl.when(same)
        def _():
            lax.fori_loop(0, nz // 2 - (1 if nz // 2 % 2 == 0 else 0), one, 0)

        @pl.when(jnp.logical_not(same))
        def _():
            lax.fori_loop(0, nz // 2 - (1 if nz // 2 % 2 else 0), other, 0)

    def rows(i):
        return pl.ds(pl.multiple_of(((i % 2) * (nz // 2) + i // 2) * ch, ch), ch)

    def half(p):
        return pl.ds(p * HALF, HALF)

    def bulk(ref, sem):
        return rcopy(ref, ref, sem, sem, xdev(xat(1)))

    def cols(h):
        return pl.ds(h * E if isinstance(h, int) else pl.multiple_of(h * E, E), E)

    loads = [
        pltpu.make_async_copy(a, b, in_s.at[i])
        for i, (a, b) in enumerate(((ki, k), (vi, v), (qi, q), (ogi, og), (ldi, ld), (gaini, gain)))
    ]
    for i in (4, 0, 1, 2, 3, 5):
        loads[i].start()
    barrier = pltpu.get_barrier_semaphore()
    for n in range(1, NX):
        pl.semaphore_signal(barrier, inc=1, device_id=xdev(xat(n)), device_id_type=MESH)
    each(nz, lambda i: pl.semaphore_signal(barrier, inc=1, device_id=zdev(zat(i)), device_id_type=MESH))
    each(nd, lambda i: pl.semaphore_signal(barrier, inc=1, device_id=ddev(dat(i)), device_id_type=MESH))

    first = lax.broadcasted_iota(jnp.int32, (E, E), 0)
    second = lax.broadcasted_iota(jnp.int32, (E, E), 1)
    upper = jnp.where(first <= second, 1.0, 0.0).astype(F32)
    causal = second <= first
    loads[4].wait()
    cum = lax.dot_general(
        ld[...], upper, (((1,), (0,)), ((), ())),
        precision=lax.Precision.HIGHEST, preferred_element_type=F32,
    )
    end = cum[:, E - 1:E]
    dself[...] = jnp.exp(jnp.broadcast_to(end, (HEADS, E)))
    cum_col = cum.T
    fs_col = jnp.exp(cum).T
    te_col = jnp.exp(end - cum).T
    for h in range(HEADS):
        fs[h] = jnp.broadcast_to(fs_col[:, h:h + 1], (E, E))
        te[h] = jnp.broadcast_to(te_col[:, h:h + 1], (E, E))

    loads[0].wait()
    loads[1].wait()
    for j in range(PER):
        for n in (2, 1, 3, 0):
            h = PER * xat(n) + j
            kd = (k[:, cols(h)].astype(F32) * te[h]).astype(BF16)
            state = dot(kd, v[:, cols(h)], 0, 0)
            if n:
                st[0, h] = state
            else:
                xr[0, j, x] = state
    dx[x] = dself[...]

    pl.semaphore_wait(barrier, NX - 1 + nz - 1 + nd - 1)

    def dx_copy(i, slot):
        return rcopy(dself, dx.at[slot], dx_s.at[i], dx_r.at[slot], xdev(i))

    def dz_copy(i, slot):
        return rcopy(drow, dz.at[slot], dz_s.at[0], dz_r.at[0], zdev(i))

    def xs_copy(d, j, p, i, slot):
        return rcopy(
            st.at[d, PER * i + j, half(p)], xr.at[d, j, slot, half(p)],
            xs_s.at[j, p, i], xs_r.at[d, j, p, slot], xdev(i),
        )

    def zs_copy(d, j, i, slot):
        return rcopy(rt.at[d, j, rows(i)], zr.at[d, j, slot], zs_s.at[d, j], zs_r.at[d, j], zdev(i))

    def zb_copy(d, j, i, slot):
        return rcopy(zp.at[d, j, i], zb.at[d, j, rows(slot)], zb_s.at[d, j], zb_r.at[d, j], zdev(i))

    def xb_copy(d, j, p, i, slot):
        return rcopy(
            ex.at[d, j, i, half(p)], eb.at[d, PER * slot + j, half(p)],
            xb_s.at[j, p, i], xb_r.at[d, j, p, slot], xdev(i),
        )

    def gx_copy(i, slot):
        return rcopy(gt, gx.at[slot], dx_s.at[i], gx_r.at[slot], xdev(i))

    def gz_copy(i, slot):
        return rcopy(gxs.at[pl.ds(i // (nz // HEADS), 1)] if nz >= HEADS else gxs.at[pl.ds(i * (HEADS // nz), 1)],
                     gz.at[slot], dz_s.at[1], gz_r.at[0], zdev(i))

    def gd_copy(i, slot):
        return rcopy(gzs, gd.at[slot], gd_s.at[0], gd_r.at[0], ddev(i))

    for n in AWAY:
        dx_copy(xat(n), x).start()
    for j in range(PER):
        for p in range(2):
            for n in AWAY:
                xs_copy(0, j, p, xat(n), x).start()

    def decay(i, j):
        return dx[i, pl.ds(PER * x + j, 1), :]

    def scan(d, fill):
        steps = range(NX) if d == 0 else range(NX - 1, -1, -1)
        for j in range(PER):
            for p in range(2):
                for n in (1, 3, 2):
                    xs_copy(d, j, p, xat(n), xat(n)).wait_recv()
                total = None
                for i in steps:
                    part = xr[d, j, i, half(p)]
                    total = part if total is None else decay(i, j) * total + part
                rt[d, j, half(p)] = total
                owners(p, lambda i: zs_copy(d, j, i, z).start())
            zr[d, j, z] = rt[d, j, rows(z)]
            fill()
        for j in range(PER):
            bulk(zr.at[d, j, pl.ds(0, nz - 1)], zs_r.at[d, j]).wait_recv()
            run = jnp.zeros((ch, E), F32)
            for s in range(nz):
                i = s if d == 0 else nz - 1 - s
                zp[d, j, i] = run
                if s < nz - 1:
                    run = dz[i, j:j + 1, :] * run + zr[d, j, i]
            far(lambda i: zb_copy(d, j, i, z).start())
            zb[d, j, rows(z)] = zp[d, j, z]
            fill()
        for j in range(PER):
            bulk(zb.at[d, j, pl.ds(0, (nz - 1) * ch)], zb_r.at[d, j]).wait_recv()
            for p in range(2):
                carried = zb[d, j, half(p)]
                for s, i in enumerate(steps):
                    ex[d, j, i, half(p)] = carried
                    if s < NX - 1:
                        carried = decay(i, j) * carried + xr[d, j, i, half(p)]
                for n in AWAY:
                    xb_copy(d, j, p, xat(n), x).start()
            eb[d, PER * x + j] = ex[d, j, x]

    def sent(d):
        for j in range(PER):
            for p in range(2):
                for n in AWAY:
                    xs_copy(d, j, p, xat(n), x).wait_send()
                    xb_copy(d, j, p, xat(n), x).wait_send()
            bulk(rt.at[d, j, pl.ds(0, (nz - 1) * ch)], zs_s.at[d, j]).wait_send()
            bulk(zp.at[d, j, pl.ds(0, nz - 1)], zb_s.at[d, j]).wait_send()

    def early(h):
        own = cum_col[:, h:h + 1] - cum[h:h + 1, :]
        mask = jnp.where(causal, jnp.exp(jnp.where(causal, own, 0.0)), 0.0)
        dm[h] = mask
        w = (dot(q[:, cols(h)], k[:, cols(h)], 1, 1) * mask).astype(BF16)
        wts[h] = w
        att[h] = dot(w, v[:, cols(h)], 1, 0)

    loads[2].wait()
    early(0)
    for n in AWAY:
        dx_copy(xat(n), xat(n)).wait_recv()
    for j in range(PER):
        drow[j:j + 1, :] = decay(0, j) * decay(1, j) * decay(2, j) * decay(3, j)
    dz[z] = drow[...]
    far(lambda i: dz_copy(i, z).start())
    early(1)
    todo = [(2, 3), (4, 5), (6,), (7,)]

    def fill_early():
        for h in todo.pop(0):
            early(h)
        if len(todo) == 2:
            bulk(dz.at[pl.ds(0, nz - 1)], dz_r.at[0]).wait_recv()

    scan(0, fill_early)

    loads[3].wait()
    loads[5].wait()
    for n in AWAY:
        dx_copy(xat(n), x).wait_send()
    for j in range(PER):
        for p in range(2):
            for n in AWAY:
                xs_copy(0, j, p, xat(n), x).wait_send()

    for j in range(PER):
        for n in NEAR:
            i = xat(n)
            h = PER * i + j
            if n:
                for p in range(2):
                    xb_copy(0, j, p, i, i).wait_recv()
            eh = eb[0, h].astype(BF16)
            qh = q[:, cols(h)]
            start = fs[h]
            attended = start * dot(qh, eh, 1, 0) + att[h]
            inverse = lax.rsqrt(jnp.mean(attended * attended, axis=-1, keepdims=True) + EPSILON)
            normed = attended * inverse
            up = og[:, cols(h)].astype(F32)
            scaled = gain[pl.ds(h, 1), :] * up
            a = (
                (scaled - normed * jnp.mean(scaled * normed, axis=-1, keepdims=True)) * inverse
            ).astype(BF16)
            ag[h] = a
            qd = (qh.astype(F32) * start).astype(BF16)
            adjoint = dot(qd, a, 0, 0)
            if n:
                st[1, h] = adjoint
                for p in range(2):
                    xs_copy(1, j, p, i, x).start()
            else:
                xr[1, j, x] = adjoint
            gt[pl.ds(h, 1), :] = jnp.sum(up * normed, axis=0, keepdims=True)
    for n in AWAY:
        gx_copy(xat(n), x).start()
    gx[x] = gt[...]

    def late(h):
        a = ag[h]
        vh = v[:, cols(h)]
        gw = (dot(a, vh, 1, 1) * dm[h]).astype(BF16)
        eh = eb[0, h].astype(BF16)
        grad = fs[h] * dot(a, eh, 1, 1) + dot(gw, k[:, cols(h)], 1, 0)
        qg[:, cols(h)] = grad.astype(BF16)
        kgi[h] = dot(gw, q[:, cols(h)], 0, 0)
        vgi[h] = dot(wts[h], a, 0, 0)

    late(0)
    late(1)
    rest = [(2, 3), (4, 5), (6,), (7,)]

    def fill_late():
        for h in rest.pop(0):
            late(h)
        if len(rest) == 2:
            for n in AWAY:
                gx_copy(xat(n), xat(n)).wait_recv()
            gxs[...] = gx[0] + gx[1] + gx[2] + gx[3]
            far(lambda i: gz_copy(i, z).start())
            gz[z] = gxs[pl.ds(z // (nz // HEADS), 1), :] if nz >= HEADS else gxs[pl.ds(z * (HEADS // nz), 1), :]
        if len(rest) == 0:
            bulk(gz.at[pl.ds(0, nz - 1)], gz_r.at[0]).wait_recv()
            gzs[...] = jnp.sum(gz[...], axis=0)
            each(nd, lambda i: gd_copy(dat(i), me).start())
            gd[me] = gzs[...]

    for j in range(PER):
        for p in range(2):
            for n in AWAY:
                xb_copy(0, j, p, xat(n), x).wait_send()

    scan(1, fill_late)

    for j in range(PER):
        for n in NEAR:
            i = xat(n)
            h = PER * i + j
            if n:
                for p in range(2):
                    xb_copy(1, j, p, i, i).wait_recv()
            rh = eb[1, h].astype(BF16)
            stop = te[h]
            kg[:, cols(h)] = (stop * dot(v[:, cols(h)], rh, 1, 1) + kgi[h]).astype(BF16)
            vg[:, cols(h)] = (stop * dot(k[:, cols(h)], rh, 1, 0) + vgi[h]).astype(BF16)

    bulk(gd.at[pl.ds(0, nd - 1)], gd_r.at[0]).wait_recv()
    gg[...] = jnp.sum(gd[...], axis=0)

    for n in AWAY:
        gx_copy(xat(n), x).wait_send()
    bulk(dz.at[pl.ds(0, nz - 1)], dz_s.at[0]).wait_send()
    bulk(gz.at[pl.ds(0, nz - 1)], dz_s.at[1]).wait_send()
    bulk(gd.at[pl.ds(0, nd - 1)], gd_s.at[0]).wait_send()
    for j in range(PER):
        bulk(rt.at[0, j, pl.ds(0, (nz - 1) * ch)], zs_s.at[0, j]).wait_send()
        bulk(zp.at[0, j, pl.ds(0, nz - 1)], zb_s.at[0, j]).wait_send()
    sent(1)


def body(queries, keys, values, log_decay, gain, out_grad):
    nc = lax.axis_size("ctx")
    nd = lax.axis_size("dp")
    nz = nc // NX
    ch = E // nz
    width = HEADS * E

    def vm(*shape, dtype=F32):
        return pltpu.VMEM(shape, dtype)

    dma = lambda *shape: pltpu.SemaphoreType.DMA(shape)
    flat = lambda a: a.reshape(E, width)
    hbm = pltpu.HBM
    wide = jax.ShapeDtypeStruct((E, width), BF16)
    qg, kg, vg, gg = pl.pallas_call(
        functools.partial(kernel, nz, nd),
        out_shape=(wide, wide, wide, jax.ShapeDtypeStruct((1, E), F32)),
        in_specs=[pl.BlockSpec(memory_space=m) for m in [hbm] * 6],
        out_specs=tuple([pl.BlockSpec(memory_space=pltpu.VMEM)] * 4),
        scratch_shapes=[
            *[vm(E, width, dtype=BF16)] * 4, vm(HEADS, E), vm(HEADS, E),
            vm(HEADS, E, E), vm(HEADS, E, E), vm(HEADS, E, E),
            vm(HEADS, E, E, dtype=BF16), vm(HEADS, E, E), vm(HEADS, E, E, dtype=BF16),
            vm(HEADS, E, E), vm(HEADS, E, E),
            vm(HEADS, E), vm(NX, HEADS, E), vm(PER, E), vm(nz, PER, E),
            vm(2, HEADS, E, E), vm(2, PER, NX, E, E), vm(2, PER, E, E),
            vm(2, PER, nz, ch, E), vm(2, PER, nz, ch, E), vm(2, PER, E, E),
            vm(2, PER, NX, E, E), vm(2, HEADS, E, E),
            vm(HEADS, E), vm(NX, HEADS, E), vm(HEADS, E), vm(nz, 1, E),
            vm(1, E), vm(nd, 1, E),
            dma(PER, 2, NX), dma(2, PER, 2, NX), dma(2, PER), dma(2, PER),
            dma(2, PER), dma(2, PER), dma(PER, 2, NX), dma(2, PER, 2, NX),
            dma(NX), dma(NX), dma(2), dma(1), dma(1), dma(NX), dma(1), dma(1), dma(6),
        ],
        compiler_params=pltpu.CompilerParams(
            collective_id=0, has_side_effects=True, vmem_limit_bytes=48 * 1024 * 1024
        ),
    )(
        flat(queries), flat(keys), flat(values), log_decay.reshape(HEADS, E),
        gain.reshape(HEADS, E), flat(out_grad),
    )
    portion = width // nc
    share = lax.dynamic_slice_in_dim(
        gg.reshape(E), lax.axis_index("ctx") * portion % E, portion
    )
    whole = lambda a: a.reshape(1, E, width)
    return whole(qg), whole(kg), whole(vg), share


def solution(mesh):
    in_specs = (
        P("dp", "ctx", None),
        P("dp", "ctx", None),
        P("dp", "ctx", None),
        P("dp", None, "ctx"),
        P(),
        P("dp", "ctx", None),
    )
    out_specs = (P("dp", "ctx", None), P("dp", "ctx", None), P("dp", "ctx", None), P("ctx"))
    return jax.shard_map(body, mesh=mesh, in_specs=in_specs, out_specs=out_specs, check_vma=False)
```

time: 88.1 us -> 78.4 us (0.89)
  Pallas kernels: 80 us -> 70.1 us
    pallas_call x1, Pallas kernels: 80 us -> 70.1 us  [body(): pl.pallas_call(functools.partial(kernel, nz, nd), out_shape=(wide, wide,...]
where the time goes in v2:
time: 78.4 us; the launch traced here: 78 us
  Pallas kernels  70.1 us (89%)
  local copies, waits for them, and re-layouts  7.18 us (9%)
    pallas_call x1, Pallas kernels, body(): pl.pallas_call(functools.partial(kernel, nz, nd), out_shape=(wide, wide,...  70.1 us
    unnamed x15, local copies, waits for them, and re-layouts  6.59 us

profile of v2, /device:TPU:24, one launch (start us, length us, event | category | flops | bytes accessed | tf_op | source)
XLA Modules:
  0.0 78.0 jit_solution(2045604980235128243)
XLA Ops:
  0.6 0.0 copy-start.5
  0.7 0.0 copy-start.4
  0.7 0.7 copy-done.5
  1.3 0.0 copy-done.4
  1.4 0.0 copy-start
  1.4 0.9 %copy-done = bf16[1,128,1024]{2,1,0:T(8,128)(2,1)S(1)} copy-done((bf16[1,128,1024]{2,1,0:T(8,128)(2,1)S(1)}, bf16[1,128,1024]{2,1,0:T(8,128)(2,1)}, u32[]{:S(2)}) %copy-start) | copy-done | bytes 262168
  2.3 0.0 copy-start.1
  2.3 0.9 %copy-done.1 = bf16[1,128,1024]{2,1,0:T(8,128)(2,1)S(1)} copy-done((bf16[1,128,1024]{2,1,0:T(8,128)(2,1)S(1)}, bf16[1,128,1024]{2,1,0:T(8,128)(2,1)}, u32[]{:S(2)}) %copy-start.1) | copy-done | bytes 262168
  3.3 0.0 copy-start.2
  3.3 0.9 %copy-done.2 = bf16[1,128,1024]{2,1,0:T(8,128)(2,1)S(1)} copy-done((bf16[1,128,1024]{2,1,0:T(8,128)(2,1)S(1)}, bf16[1,128,1024]{2,1,0:T(8,128)(2,1)}, u32[]{:S(2)}) %copy-start.2) | copy-done | bytes 262168
  4.2 0.0 copy-start.3
  4.2 0.9 %copy-done.3 = bf16[1,128,1024]{2,1,0:T(8,128)(2,1)S(1)} copy-done((bf16[1,128,1024]{2,1,0:T(8,128)(2,1)S(1)}, bf16[1,128,1024]{2,1,0:T(8,128)(2,1)}, u32[]{:S(2)}) %copy-start.3) | copy-done | bytes 262168
  5.2 70.1 %shard_map.93 = (bf16[128,1024]{1,0:T(8,128)(2,1)S(1)}, bf16[128,1024]{1,0:T(8,128)(2,1)S(1)}, bf16[128,1024]{1,0:T(8,128)(2,1)S(1)}, f32[1,128]{1,0:T(1,128)S(1)}) custom-call(bf16[128,1024]{1,0:T(8,128)(2,1)S(1)} %bitcast.14, bf16[128,1024]{1,0:T(8,128)(2,1)S(1)} %bitcast.15, bf16[128,1024]{1,0:T(8,128)(2,1)S(1)} %bitcast.16, f32[8,128]{1,0:T(8,128)S(1)} %bitcast.18, ...), custom_call_target="tpu_custom_call" | custom-call | tf_op jit(solution)/shard_map/pallas_call | solution.py:388
  75.3 0.6 dynamic-slice_bitcast_fusion
  75.9 0.7 copy.13
  76.6 0.7 copy.14
  77.3 0.7 copy.15
Async XLA Ops:
  0.6 0.7 copy-start.5
  0.7 0.7 copy-start.4
  1.4 0.9 %copy-start = (bf16[1,128,1024]{2,1,0:T(8,128)(2,1)S(1)}, bf16[1,128,1024]{2,1,0:T(8,128)(2,1)}, u32[]{:S(2)}) copy-start(bf16[1,128,1024]{2,1,0:T(8,128)(2,1)} %param.6) | copy-start | bytes 786436
  2.3 0.9 %copy-start.1 = (bf16[1,128,1024]{2,1,0:T(8,128)(2,1)S(1)}, bf16[1,128,1024]{2,1,0:T(8,128)(2,1)}, u32[]{:S(2)}) copy-start(bf16[1,128,1024]{2,1,0:T(8,128)(2,1)} %param.7) | copy-start | bytes 786436
  3.3 0.9 %copy-start.2 = (bf16[1,128,1024]{2,1,0:T(8,128)(2,1)S(1)}, bf16[1,128,1024]{2,1,0:T(8,128)(2,1)}, u32[]{:S(2)}) copy-start(bf16[1,128,1024]{2,1,0:T(8,128)(2,1)} %param.8) | copy-start | bytes 786436
  4.2 0.9 %copy-start.3 = (bf16[1,128,1024]{2,1,0:T(8,128)(2,1)S(1)}, bf16[1,128,1024]{2,1,0:T(8,128)(2,1)}, u32[]{:S(2)}) copy-start(bf16[1,128,1024]{2,1,0:T(8,128)(2,1)} %param.11) | copy-start | bytes 786436

commit v3 on v2

--- a/solution.py
+++ b/solution.py
@@ -29,7 +29,7 @@
            dself, dx, drow, dz, st, xr, rt, zr, zp, zb, ex, eb,
            gt, gx, gxs, gz, gzs, gd,
            xs_s, xs_r, zs_s, zs_r, zb_s, zb_r, xb_s, xb_r,
-           dx_s, dx_r, dz_s, dz_r, gd_s, gx_r, gz_r, gd_r, in_s):
+           dx_s, dx_r, dz_s, dz_r, gd_s, gx_r, gz_r, gd_r, in_s, second_s, third_s):
     ch = E // nz
     c = lax.axis_index("ctx")
     me = lax.axis_index("dp")
@@ -115,7 +115,8 @@
     barrier = pltpu.get_barrier_semaphore()
     for n in range(1, NX):
         pl.semaphore_signal(barrier, inc=1, device_id=xdev(xat(n)), device_id_type=MESH)
-    each(nz, lambda i: pl.semaphore_signal(barrier, inc=1, device_id=zdev(zat(i)), device_id_type=MESH))
+    for n in (1, 2, nz - 2, nz - 1):
+        pl.semaphore_signal(barrier, inc=1, device_id=zdev(zat(n)), device_id_type=MESH)
     each(nd, lambda i: pl.semaphore_signal(barrier, inc=1, device_id=ddev(dat(i)), device_id_type=MESH))
 
     first = lax.broadcasted_iota(jnp.int32, (E, E), 0)
@@ -138,6 +139,49 @@
 
     loads[0].wait()
     loads[1].wait()
+    def dx_copy(i, slot):
+        return rcopy(dself, dx.at[slot], dx_s.at[i], dx_r.at[slot], xdev(i))
+
+    def dz_copy(i, slot):
+        return rcopy(drow, dz.at[slot], dz_s.at[0], dz_r.at[0], zdev(i))
+
+    def xs_copy(d, j, p, i, slot):
+        return rcopy(
+            st.at[d, PER * i + j, half(p)], xr.at[d, j, slot, half(p)],
+            xs_s.at[j, p, i], xs_r.at[d, j, p, slot], xdev(i),
+        )
+
+    def zs_copy(d, j, i, slot):
+        return rcopy(rt.at[d, j, rows(i)], zr.at[d, j, slot], zs_s.at[d, j], zs_r.at[d, j], zdev(i))
+
+    def zb_copy(d, j, i, slot):
+        return rcopy(zp.at[d, j, i], zb.at[d, j, rows(slot)], zb_s.at[d, j], zb_r.at[d, j], zdev(i))
+
+    def xb_copy(d, j, p, i, slot):
+        return rcopy(
+            ex.at[d, j, i, half(p)], eb.at[d, PER * slot + j, half(p)],
+            xb_s.at[j, p, i], xb_r.at[d, j, p, slot], xdev(i),
+        )
+
+    def gx_copy(i, slot):
+        return rcopy(gt, gx.at[slot], dx_s.at[i], gx_r.at[slot], xdev(i))
+
+    def gz_copy(i, slot):
+        return rcopy(gxs.at[pl.ds(i // (nz // HEADS), 1)] if nz >= HEADS else gxs.at[pl.ds(i * (HEADS // nz), 1)],
+                     gz.at[slot], dz_s.at[1], gz_r.at[0], zdev(i))
+
+    def gd_copy(i, slot):
+        return rcopy(gzs, gd.at[slot], gd_s.at[0], gd_r.at[0], ddev(i))
+
+    def tell(sem, n):
+        for m in (n, nz - n):
+            pl.semaphore_signal(sem, inc=1, device_id=zdev(zat(m)), device_id_type=MESH)
+
+    pl.semaphore_wait(barrier, NX - 1 + 4 + nd - 1)
+    tell(second_s, 2)
+    for n in AWAY:
+        dx_copy(xat(n), x).start()
+    dx[x] = dself[...]
     for j in range(PER):
         for n in (2, 1, 3, 0):
             h = PER * xat(n) + j
@@ -145,52 +189,13 @@
             state = dot(kd, v[:, cols(h)], 0, 0)
             if n:
                 st[0, h] = state
+                for p in range(2):
+                    xs_copy(0, j, p, xat(n), x).start()
             else:
                 xr[0, j, x] = state
-    dx[x] = dself[...]
-
-    pl.semaphore_wait(barrier, NX - 1 + nz - 1 + nd - 1)
-
-    def dx_copy(i, slot):
-        return rcopy(dself, dx.at[slot], dx_s.at[i], dx_r.at[slot], xdev(i))
-
-    def dz_copy(i, slot):
-        return rcopy(drow, dz.at[slot], dz_s.at[0], dz_r.at[0], zdev(i))
-
-    def xs_copy(d, j, p, i, slot):
-        return rcopy(
-            st.at[d, PER * i + j, half(p)], xr.at[d, j, slot, half(p)],
-            xs_s.at[j, p, i], xs_r.at[d, j, p, slot], xdev(i),
-        )
-
-    def zs_copy(d, j, i, slot):
-        return rcopy(rt.at[d, j, rows(i)], zr.at[d, j, slot], zs_s.at[d, j], zs_r.at[d, j], zdev(i))
-
-    def zb_copy(d, j, i, slot):
-        return rcopy(zp.at[d, j, i], zb.at[d, j, rows(slot)], zb_s.at[d, j], zb_r.at[d, j], zdev(i))
-
-    def xb_copy(d, j, p, i, slot):
-        return rcopy(
-            ex.at[d, j, i, half(p)], eb.at[d, PER * slot + j, half(p)],
-            xb_s.at[j, p, i], xb_r.at[d, j, p, slot], xdev(i),
-        )
-
-    def gx_copy(i, slot):
-        return rcopy(gt, gx.at[slot], dx_s.at[i], gx_r.at[slot], xdev(i))
-
-    def gz_copy(i, slot):
-        return rcopy(gxs.at[pl.ds(i // (nz // HEADS), 1)] if nz >= HEADS else gxs.at[pl.ds(i * (HEADS // nz), 1)],
-                     gz.at[slot], dz_s.at[1], gz_r.at[0], zdev(i))
-
-    def gd_copy(i, slot):
-        return rcopy(gzs, gd.at[slot], gd_s.at[0], gd_r.at[0], ddev(i))
-
-    for n in AWAY:
-        dx_copy(xat(n), x).start()
-    for j in range(PER):
-        for p in range(2):
-            for n in AWAY:
-                xs_copy(0, j, p, xat(n), x).start()
+    pl.semaphore_wait(second_s, 2)
+    if nz > 8:
+        tell(third_s, 4)
 
     def decay(i, j):
         return dx[i, pl.ds(PER * x + j, 1), :]
@@ -253,6 +258,8 @@
     early(0)
     for n in AWAY:
         dx_copy(xat(n), xat(n)).wait_recv()
+    if nz > 8:
+        pl.semaphore_wait(third_s, 2)
     for j in range(PER):
         drow[j:j + 1, :] = decay(0, j) * decay(1, j) * decay(2, j) * decay(3, j)
     dz[z] = drow[...]
@@ -371,6 +378,22 @@
     sent(1)
 
 
+def write(qv, kv, vv, row, qo, ko, vo, share, held, sems):
+    arrays = ((qv, qo), (kv, ko), (vv, vo))
+    reads = [pltpu.make_async_copy(a, held.at[i], sems.at[0, i]) for i, (a, _) in enumerate(arrays)]
+    writes = [pltpu.make_async_copy(held.at[i], b, sems.at[1, i]) for i, (_, b) in enumerate(arrays)]
+    for read in reads:
+        read.start()
+    portion = share.shape[1]
+    at = lax.rem(lax.axis_index("ctx") * portion, E)
+    share[...] = pltpu.roll(row[...], lax.rem(E - at, E), 1)[:, :portion]
+    for read, put in zip(reads, writes):
+        read.wait()
+        put.start()
+    for put in writes:
+        put.wait()
+
+
 def body(queries, keys, values, log_decay, gain, out_grad):
     nc = lax.axis_size("ctx")
     nd = lax.axis_size("dp")
@@ -404,20 +427,28 @@
             dma(PER, 2, NX), dma(2, PER, 2, NX), dma(2, PER), dma(2, PER),
             dma(2, PER), dma(2, PER), dma(PER, 2, NX), dma(2, PER, 2, NX),
             dma(NX), dma(NX), dma(2), dma(1), dma(1), dma(NX), dma(1), dma(1), dma(6),
+            pltpu.SemaphoreType.REGULAR, pltpu.SemaphoreType.REGULAR,
         ],
         compiler_params=pltpu.CompilerParams(
-            collective_id=0, has_side_effects=True, vmem_limit_bytes=48 * 1024 * 1024
+            collective_id=0, has_side_effects=True, vmem_limit_bytes=66150000
         ),
     )(
         flat(queries), flat(keys), flat(values), log_decay.reshape(HEADS, E),
         gain.reshape(HEADS, E), flat(out_grad),
     )
     portion = width // nc
-    share = lax.dynamic_slice_in_dim(
-        gg.reshape(E), lax.axis_index("ctx") * portion % E, portion
-    )
+    vmem = pl.BlockSpec(memory_space=pltpu.VMEM)
+    away = pl.BlockSpec(memory_space=hbm)
+    qg, kg, vg, share = pl.pallas_call(
+        write,
+        out_shape=(wide, wide, wide, jax.ShapeDtypeStruct((1, portion), F32)),
+        in_specs=[pl.BlockSpec(memory_space=pl.ANY)] * 3 + [vmem],
+        out_specs=(away, away, away, vmem),
+        scratch_shapes=[vm(3, E, width, dtype=BF16), pltpu.SemaphoreType.DMA((2, 3))],
+        compiler_params=pltpu.CompilerParams(vmem_limit_bytes=66150000),
+    )(qg, kg, vg, gg)
     whole = lambda a: a.reshape(1, E, width)
-    return whole(qg), whole(kg), whole(vg), share
+    return whole(qg), whole(kg), whole(vg), share.reshape(portion)
 
 
 def solution(mesh):

time: 78.4 us -> 74.1 us (0.945)
  local copies, waits for them, and re-layouts: 7.18 us -> 0 us
  Pallas kernels: 70.1 us -> 72.6 us
    unnamed x15 -> x0, local copies, waits for them, and re-layouts: 6.59 us -> none
    pallas_call x0 -> x1, Pallas kernels: none -> 3.01 us  [body(): pl.pallas_call(write, out_shape=(wide, wide, wide, jax.ShapeDtypeStruct((...]
where the time goes in v3:
time: 74.1 us; the launch traced here: 73.2 us
  Pallas kernels  72.6 us (98%)
    pallas_call x1, Pallas kernels, body(): pl.pallas_call(functools.partial(kernel, nz, nd), out_shape=(wide, wide,...  69.6 us
    pallas_call x1, Pallas kernels, body(): pl.pallas_call(write, out_shape=(wide, wide, wide, jax.ShapeDtypeStruct((...  3.01 us

profile of v3, /device:TPU:24, one launch (start us, length us, event | category | flops | bytes accessed | tf_op | source)
XLA Modules:
  0.0 73.2 jit_solution(10206988790467694038)
XLA Ops:
  0.6 69.6 %shard_map.93 = (bf16[128,1024]{1,0:T(8,128)(2,1)}, bf16[128,1024]{1,0:T(8,128)(2,1)}, bf16[128,1024]{1,0:T(8,128)(2,1)}, f32[1,128]{1,0:T(1,128)}) custom-call(bf16[128,1024]{1,0:T(8,128)(2,1)} %bitcast.10, bf16[128,1024]{1,0:T(8,128)(2,1)} %bitcast.11, bf16[128,1024]{1,0:T(8,128)(2,1)} %bitcast.12, f32[8,128]{1,0:T(8,128)} %bitcast.14, f32[8,128]{1,0:T(8,128)} %bitcast.15, ...), custom_call_target="tpu_custom_call" | custom-call | tf_op jit(solution)/shard_map/pallas_call | solution.py:411
  70.2 3.0 %shard_map.94 = (bf16[128,1024]{1,0:T(8,128)(2,1)}, bf16[128,1024]{1,0:T(8,128)(2,1)}, bf16[128,1024]{1,0:T(8,128)(2,1)}, f32[1,16]{1,0:T(1,128)}) custom-call(bf16[128,1024]{1,0:T(8,128)(2,1)} %get-tuple-element.12.qv, bf16[128,1024]{1,0:T(8,128)(2,1)} %get-tuple-element.13.kv, bf16[128,1024]{1,0:T(8,128)(2,1)} %get-tuple-element.14.vv, ...), custom_call_target="tpu_custom_call" | custom-call | tf_op jit(solution)/shard_map/pallas_call | solution.py:442

commit v4 on v3

--- a/solution.py
+++ b/solution.py
@@ -24,12 +24,12 @@
     return lax.dot_general(a, b, (((ca,), (cb,)), ((), ())), preferred_element_type=F32)
 
 
-def kernel(nz, nd, qi, ki, vi, ldi, gaini, ogi, qg, kg, vg, gg, q, k, v, og, ld, gain,
+def kernel(nz, nd, qi, ki, vi, ldi, gaini, ogi, qo, ko, vo, gg, qg, kg, vg, q, k, v, og, ld, gain,
            fs, te, dm, wts, att, ag, kgi, vgi,
            dself, dx, drow, dz, st, xr, rt, zr, zp, zb, ex, eb,
            gt, gx, gxs, gz, gzs, gd,
            xs_s, xs_r, zs_s, zs_r, zb_s, zb_r, xb_s, xb_r,
-           dx_s, dx_r, dz_s, dz_r, gd_s, gx_r, gz_r, gd_r, in_s, second_s, third_s):
+           dx_s, dx_r, dz_s, dz_r, gd_s, gx_r, gz_r, gd_r, in_s, second_s, third_s, out_s):
     ch = E // nz
     c = lax.axis_index("ctx")
     me = lax.axis_index("dp")
@@ -351,6 +351,8 @@
                 xb_copy(0, j, p, xat(n), x).wait_send()
 
     scan(1, fill_late)
+    outs = [pltpu.make_async_copy(a, b, out_s.at[i]) for i, (a, b) in enumerate(((qg, qo), (kg, ko), (vg, vo)))]
+    outs[0].start()
 
     for j in range(PER):
         for n in NEAR:
@@ -364,6 +366,8 @@
             kg[:, cols(h)] = (stop * dot(v[:, cols(h)], rh, 1, 1) + kgi[h]).astype(BF16)
             vg[:, cols(h)] = (stop * dot(k[:, cols(h)], rh, 1, 0) + vgi[h]).astype(BF16)
 
+    outs[1].start()
+    outs[2].start()
     bulk(gd.at[pl.ds(0, nd - 1)], gd_r.at[0]).wait_recv()
     gg[...] = jnp.sum(gd[...], axis=0)
 
@@ -376,6 +380,8 @@
         bulk(rt.at[0, j, pl.ds(0, (nz - 1) * ch)], zs_s.at[0, j]).wait_send()
         bulk(zp.at[0, j, pl.ds(0, nz - 1)], zb_s.at[0, j]).wait_send()
     sent(1)
+    for out in outs:
+        out.wait()
 
 
 def write(qv, kv, vv, row, qo, ko, vo, share, held, sems):
@@ -412,9 +418,9 @@
         functools.partial(kernel, nz, nd),
         out_shape=(wide, wide, wide, jax.ShapeDtypeStruct((1, E), F32)),
         in_specs=[pl.BlockSpec(memory_space=m) for m in [hbm] * 6],
-        out_specs=tuple([pl.BlockSpec(memory_space=pltpu.VMEM)] * 4),
+        out_specs=tuple(pl.BlockSpec(memory_space=m) for m in (hbm, hbm, hbm, pltpu.VMEM)),
         scratch_shapes=[
-            *[vm(E, width, dtype=BF16)] * 4, vm(HEADS, E), vm(HEADS, E),
+            *[vm(E, width, dtype=BF16)] * 7, vm(HEADS, E), vm(HEADS, E),
             vm(HEADS, E, E), vm(HEADS, E, E), vm(HEADS, E, E),
             vm(HEADS, E, E, dtype=BF16), vm(HEADS, E, E), vm(HEADS, E, E, dtype=BF16),
             vm(HEADS, E, E), vm(HEADS, E, E),
@@ -427,7 +433,7 @@
             dma(PER, 2, NX), dma(2, PER, 2, NX), dma(2, PER), dma(2, PER),
             dma(2, PER), dma(2, PER), dma(PER, 2, NX), dma(2, PER, 2, NX),
             dma(NX), dma(NX), dma(2), dma(1), dma(1), dma(NX), dma(1), dma(1), dma(6),
-            pltpu.SemaphoreType.REGULAR, pltpu.SemaphoreType.REGULAR,
+            pltpu.SemaphoreType.REGULAR, pltpu.SemaphoreType.REGULAR, dma(3),
         ],
         compiler_params=pltpu.CompilerParams(
             collective_id=0, has_side_effects=True, vmem_limit_bytes=66150000

time: 74.1 us -> 74.6 us (level)
  no operation moved by 1% of the time
where the time goes in v4:
time: 74.6 us; the launch traced here: 73.6 us
  Pallas kernels  72.9 us (98%)
    pallas_call x1, Pallas kernels, body(): pl.pallas_call(functools.partial(kernel, nz, nd), out_shape=(wide, wide,...  69.9 us
    pallas_call x1, Pallas kernels, body(): pl.pallas_call(write, out_shape=(wide, wide, wide, jax.ShapeDtypeStruct((...  3.01 us

profile of v4, /device:TPU:24, one launch (start us, length us, event | category | flops | bytes accessed | tf_op | source)
XLA Modules:
  0.0 73.6 jit_solution(15202268137734999307)
XLA Ops:
  0.6 69.9 %shard_map.93 = (bf16[128,1024]{1,0:T(8,128)(2,1)}, bf16[128,1024]{1,0:T(8,128)(2,1)}, bf16[128,1024]{1,0:T(8,128)(2,1)}, f32[1,128]{1,0:T(1,128)}) custom-call(bf16[128,1024]{1,0:T(8,128)(2,1)} %bitcast.10, bf16[128,1024]{1,0:T(8,128)(2,1)} %bitcast.11, bf16[128,1024]{1,0:T(8,128)(2,1)} %bitcast.12, f32[8,128]{1,0:T(8,128)} %bitcast.14, f32[8,128]{1,0:T(8,128)} %bitcast.15, ...), custom_call_target="tpu_custom_call" | custom-call | tf_op jit(solution)/shard_map/pallas_call | solution.py:417
  70.6 3.0 %shard_map.94 = (bf16[128,1024]{1,0:T(8,128)(2,1)}, bf16[128,1024]{1,0:T(8,128)(2,1)}, bf16[128,1024]{1,0:T(8,128)(2,1)}, f32[1,16]{1,0:T(1,128)}) custom-call(bf16[128,1024]{1,0:T(8,128)(2,1)} %get-tuple-element.12.qv, bf16[128,1024]{1,0:T(8,128)(2,1)} %get-tuple-element.13.kv, bf16[128,1024]{1,0:T(8,128)(2,1)} %get-tuple-element.14.vv, ...), custom_call_target="tpu_custom_call" | custom-call | tf_op jit(solution)/shard_map/pallas_call | solution.py:448
